TPU v7x, 32 devices: a whole 2x2x4 slice. The times are simulated.
32 devices in a mesh: grp: 2 (over x), seq: 16 (over z, y, core).
Axes of the slice: x: 2, y: 2, z: 4, core: 2. Of those that a mesh axis runs over, the one named last changes fastest.
Arguments:
- queries: bfloat16 [8192, 8192], P(('grp', 'seq')), parts along dimension 0, may hold values from -6 to 6
- keys_in: bfloat16 [8192, 8192], P(('grp', 'seq')), parts along dimension 0, may hold values from -0.375 to 0.375
- values_in: bfloat16 [8192, 8192], P(('grp', 'seq')), parts along dimension 0, may hold values from -6 to 6
- log_decay: bfloat16 [8192, 64], P(('grp', 'seq')), parts along dimension 0, may hold values from -2 to 0, as said below
- gate_logits: bfloat16 [8192, 8192], P(('grp', 'seq')), parts along dimension 0, may hold values from -6 to 6
- norm_gain: float32 [8192], replicated, may hold values from 0.1 to 1.9
- doc_lengths: int32 [16], P('grp'), parts along dimension 0, may hold values from 1 to 2048, 4096 in all
Outputs:
- attended: bfloat16 [8192, 8192], P(('grp', 'seq')), parts along dimension 0
- final_state: float32 [128, 128, 128], P(('grp', 'seq')), parts along dimension 0
There are 2 independent parts, one for each index of `grp`. A program takes and returns all parts, laid end to end along the dimension named above; an argument that names none is the same for every part. Nothing has to cross between parts.
Inputs may be any that keep to these rules, and one draw needn't show every extreme that they name: log_decay is negative. `doc_lengths`: the 8 lengths are positive and sum to 4096.
All inputs are finite; a program needn't handle non-finite values.
Results may differ from a plain program's by a relative error of at most 0.0049.
Values may be sent and summed in bfloat16 or wider, within the bound.
A program may use at most 320 MiB of HBM per device.

v0:
```python
import functools
import math

import jax
import jax.numpy as jnp
from jax import lax
from jax.experimental import pallas as pl
from jax.experimental.pallas import tpu as pltpu
from jax.sharding import PartitionSpec as P

EPS = 1e-05
LOG2E = 1.4426950408889634
D = 128
GROUP = 4
CHUNKS = 8
INSIDE_LAG = 2
CHAIN_LAG = 4
HOP_LAG = 2
E_LAG = 4
X_LAG = 2
FINISH_PARTS = 2
F32, BF16 = jnp.float32, jnp.bfloat16
MESH = pl.DeviceIdType.MESH


def dot(a, b, dims):
    return lax.dot_general(a, b, (dims, ((), ())), preferred_element_type=F32)


def kernel(
    n, heads, chunks,
    q_hbm, k_hbm, v_hbm, g_hbm, ld_ref, gain_ref, docs_ref,
    mix_hbm, ssq_s, fin_s,
    mix_s, q_s, k_s, v_s, g_s, pen_s, cumt_s, cumc_s, coef_s,
    fac_own, fac_s, u_own, u_core, u_mine, u_send, u_pair, s_in, s_out, e_send, e_half, x_send, ent,
    load_sem, out_sem, fac_ss, fac_rs, core_ss, core_rs, pair_ss, pair_rs, z_ss, z_rs, e_ss, e_rs,
    x_ss, x_rs, f_ss, f_rs, f_ls,
):
    tok = q_hbm.shape[0]
    hc = heads // chunks
    half = hc // 2
    w = half // 2
    planes = n // GROUP
    hn = heads // n
    g = math.gcd(w, hn)
    me = lax.axis_index("seq")
    plane = me // GROUP
    r = me % GROUP
    y = r // 2
    c = r % 2
    core_peer = plane * GROUP + y * 2 + (1 - c)
    pair_peer = plane * GROUP + (1 - y) * 2 + c

    def send(src, dst, ss, rs, dev):
        return pltpu.make_async_remote_copy(
            src_ref=src, dst_ref=dst, send_sem=ss, recv_sem=rs,
            device_id={"seq": dev}, device_id_type=MESH,
        )

    barrier = pltpu.get_barrier_semaphore()

    def greet(i, carry):
        pl.semaphore_signal(barrier, inc=1, device_id={"seq": (me + i) % n}, device_id_type=MESH)
        return carry

    lax.fori_loop(1, n, greet, 0)

    def cols(j):
        return pl.ds(pl.multiple_of(j * (hc * D), hc * D), hc * D)

    def load(which, hbm, vm, j):
        return pltpu.make_async_copy(hbm.at[:, cols(j)], vm.at[:, cols(j)], load_sem.at[which, j])

    loads = ((k_hbm, k_s), (v_hbm, v_s), (q_hbm, q_s), (g_hbm, g_s))

    def start_kv(j, carry):
        load(0, k_hbm, k_s, j).start()
        load(1, v_hbm, v_s, j).start()
        return carry

    def start_qg(j, carry):
        load(2, q_hbm, q_s, j).start()
        load(3, g_hbm, g_s, j).start()
        return carry

    lax.fori_loop(0, chunks, start_kv, 0)
    lax.fori_loop(0, chunks, start_qg, 0)

    n_docs = docs_ref.shape[0]
    rows = lax.broadcasted_iota(jnp.int32, (tok, D), 0)
    lanes = lax.broadcasted_iota(jnp.int32, (1, tok), 1)
    base = me * tok
    doc_col = jnp.zeros((tok, D), jnp.int32)
    doc_row = jnp.zeros((1, tok), jnp.int32)
    before = jnp.int32(0)
    last = jnp.int32(0)
    end = jnp.int32(0)
    for d in range(n_docs):
        end = end + docs_ref[d]
        doc_col = doc_col + jnp.where(rows + base >= end, 1, 0)
        doc_row = doc_row + jnp.where(lanes + base >= end, 1, 0)
        before = before + jnp.where(base - 1 >= end, 1, 0)
        last = last + jnp.where(base + tok - 1 >= end, 1, 0)
    causal = lax.broadcasted_iota(jnp.int32, (tok, tok), 0) >= lax.broadcasted_iota(jnp.int32, (tok, tok), 1)
    pen_s[...] = jnp.where(causal & (doc_col[:, :1] == doc_row), 0.0, -1e30).astype(F32)
    tri = jnp.where(causal, 1.0, 0.0).astype(BF16)
    ld = ld_ref[...]
    cum = dot(tri, ld, ((1,), (1,)))
    cumt = dot(ld, tri, ((1,), (1,)))
    cumt_s[...] = LOG2E * cumt
    carried = jnp.where(doc_col[:, :heads] == before, 1.0, 0.0).astype(F32)
    closing = jnp.where(doc_col[:, :heads] == last, 1.0, 0.0).astype(F32)
    lead = carried * jnp.exp(cum)
    kw = closing * jnp.exp(cum[tok - 1:tok, :] - cum)
    for j in range(chunks):
        at = slice(j * hc, (j + 1) * hc)
        coef_s[j, :, 0:hc] = lead[:, at]
        coef_s[j, :, hc:2 * hc] = kw[:, at]
    for i in range(2 * chunks):
        cumc_s[i] = LOG2E * cum[:, i * half:(i + 1) * half]
    own_f = jnp.where(last == before, 1.0, 0.0).astype(F32) * jnp.exp(
        jnp.broadcast_to(cumt[:, tok - 1:tok], (heads, D))
    )
    fac_own[...] = own_f
    fac_s[r] = own_f

    @pl.when(plane == 0)
    def _():
        s_in[...] = jnp.zeros_like(s_in)

    def lane(t):
        return slice(t * D, (t + 1) * D)

    def hcol(j, t):
        return pl.ds(pl.multiple_of(j * (hc * D) + t * D, D), D)

    def updates(j):
        load(0, k_hbm, k_s, j).wait()
        load(1, v_hbm, v_s, j).wait()
        kwj = coef_s[j, :, hc:2 * hc]
        for t in range(hc):
            kk = k_s[:, hcol(j, t)].astype(F32)
            wk = (kk * kwj[:, t:t + 1]).astype(BF16)
            up = dot(wk, v_s[:, hcol(j, t)], ((0,), (0,)))
            u_own[j, t // half, (t % half) // w, t % w] = up.astype(BF16)

    def frow(slot, h):
        return fac_s[slot, pl.ds(h, 1), :]

    def core_copy(j):
        return send(u_own.at[j, 1 - c], u_core.at[j], core_ss.at[j], core_rs.at[j], core_peer)

    def pair_copy(j):
        return send(u_send.at[j], u_pair.at[j], pair_ss.at[j], pair_rs.at[j], pair_peer)

    def combine(j):
        core_copy(j).wait_recv()
        for k in range(w):
            for mine in (True, False):
                yo = y if mine else 1 - y
                h = j * hc + c * half + yo * w + k
                f1 = frow(2 * y + 1, h)
                fa = jnp.where(c == 0, f1, 1.0)
                fb = jnp.where(c == 0, 1.0, f1)
                val = fa * u_own[j, c, yo, k].astype(F32) + fb * u_core[j, yo, k].astype(F32)
                if mine:
                    u_mine[j, k] = val
                else:
                    u_send[j, k] = val.astype(BF16)
        pair_copy(j).start()

    def z_copy(j):
        return send(s_out.at[j], s_in.at[j], z_ss.at[j], z_rs.at[j], (me + GROUP) % n)

    def e_copy(j):
        return send(e_send.at[j], e_half.at[j, y], e_ss.at[j], e_rs.at[j], pair_peer)

    def fin_place(j, s):
        h0 = j * hc + c * half + y * w + s * g
        return h0 // hn, h0 % hn

    def fin_copy(j, s):
        dev, off = fin_place(j, s)
        return send(
            s_out.at[j, pl.ds(s * g, g)], fin_s.at[pl.ds(off, g)],
            f_ss.at[j, s], f_rs.at[off // g], dev,
        )

    def fin_local(j, s):
        _, off = fin_place(j, s)
        return pltpu.make_async_copy(s_out.at[j, pl.ds(s * g, g)], fin_s.at[pl.ds(off, g)], f_ls)

    def chain(j):
        pair_copy(j).wait_recv()

        @pl.when(plane > 0)
        def _():
            z_copy(j).wait_recv()

        for k in range(w):
            h = j * hc + c * half + y * w + k
            f01 = frow(0, h) * frow(1, h)
            f23 = frow(2, h) * frow(3, h)
            mine = u_mine[j, k]
            other = u_pair[j, k].astype(F32)
            entry = s_in[j, k].astype(F32)
            mid = f01 * entry + jnp.where(y == 0, mine, other)
            s_out[j, k] = (f23 * mid + jnp.where(y == 0, other, mine)).astype(BF16)
            e_send[j, k] = jnp.where(y == 0, mid, entry).astype(BF16)
            e_half[j, y, k] = jnp.where(y == 0, entry, mid).astype(BF16)

        @pl.when(plane < planes - 1)
        def _():
            z_copy(j).start()

        @pl.when(plane == planes - 1)
        def _():
            for s in range(w // g):
                dev, _off = fin_place(j, s)

                @pl.when(dev != me)
                def _():
                    fin_copy(j, s).start()

                @pl.when(dev == me)
                def _():
                    fin_local(j, s).start()
                    fin_local(j, s).wait()

    def inside(i):
        j = i // 2

        @pl.when(i % 2 == 0)
        def _():
            load(2, q_hbm, q_s, j).wait()

        ci = cumc_s[i]
        blk = tok // 2

        for t in range(half):
            at_h = pl.ds(pl.multiple_of(i * (half * D) + t * D, D), D)
            row = cumt_s[pl.ds(i * half + t, 1), :]
            scores = dot(q_s[:, at_h], k_s[:, at_h], ((1,), (1,)))
            low = ci[:blk, t:t + 1] - row[:, :blk]
            top = (scores[:blk, :blk] * jnp.exp2(low + pen_s[:blk, :blk])).astype(BF16)
            bot = (scores[blk:] * jnp.exp2((ci[blk:, t:t + 1] - row) + pen_s[blk:, :])).astype(BF16)
            top = jnp.concatenate([top, jnp.zeros_like(top)], axis=1)
            wt = jnp.concatenate([top, bot], axis=0)
            mix_s[:, at_h] = dot(wt, v_s[:, at_h], ((1,), (0,)))

    def x_copy(j):
        return send(x_send.at[j], ent.at[j, c], x_ss.at[j], x_rs.at[j], core_peer)

    def spread(j):
        e_copy(j).wait_recv()
        for yo in range(2):
            for k in range(w):
                h = j * hc + c * half + yo * w + k
                first = e_half[j, yo, k]
                u0 = jnp.where(c == 0, u_own[j, 0, yo, k], u_core[j, yo, k]).astype(F32)
                second = (frow(2 * y, h) * first.astype(F32) + u0).astype(BF16)
                ent[j, c, yo, k] = jnp.where(c == 0, first, second)
                x_send[j, yo, k] = jnp.where(c == 0, second, first)
        x_copy(j).start()

    def store(j):
        return pltpu.make_async_copy(g_s.at[:, cols(j)], mix_hbm.at[:, cols(j)], out_sem.at[j])

    def across(j):
        x_copy(j).wait_recv()
        load(3, g_hbm, g_s, j).wait()
        lj = coef_s[j, :, 0:hc]
        acc = ssq_s[...]
        for t in range(hc):
            st = ent[j, t // half, (t % half) // w, t % w]
            mixed = mix_s[:, hcol(j, t)] + lj[:, t:t + 1] * dot(q_s[:, hcol(j, t)], st, ((1,), (0,)))
            acc = acc + mixed * mixed
            gate = g_s[:, hcol(j, t)].astype(F32)
            g_s[:, hcol(j, t)] = (mixed * (gain_ref[:, hcol(j, t)] * (0.5 * jnp.tanh(0.5 * gate) + 0.5))).astype(BF16)
        ssq_s[...] = acc
        store(j).start()

    def fac_copy(d):
        return send(fac_own, fac_s.at[r], fac_ss.at[d - 1], fac_rs.at[d - 1], plane * GROUP + (r + d) % GROUP)

    updates(0)
    pl.semaphore_wait(barrier, n - 1)
    for d in range(1, GROUP):
        fac_copy(d).start()
    core_copy(0).start()
    ssq_s[...] = jnp.zeros_like(ssq_s)
    updates(1)
    core_copy(1).start()
    for d in range(1, GROUP):
        fac_copy(d).wait_recv()
    combine(0)

    chain_lag = CHAIN_LAG + HOP_LAG * plane
    e_lag = CHAIN_LAG + HOP_LAG * (planes - 1)
    spread_lag = e_lag + E_LAG
    across_lag = spread_lag + X_LAG
    steps = max(chunks + across_lag, 2 * chunks + INSIDE_LAG)

    def step(t, carry):
        def at(lag, count, body):
            @pl.when((t >= lag) & (t < lag + count))
            def _():
                body(t - lag)

        def first(j):
            updates(j)
            core_copy(j).start()

        at(1, chunks, combine)
        at(chain_lag, chunks, chain)
        at(e_lag, chunks, lambda j: e_copy(j).start())
        at(spread_lag, chunks, spread)
        at(0, chunks, first)
        at(INSIDE_LAG, 2 * chunks, inside)
        at(across_lag, chunks, across)
        return carry

    lax.fori_loop(2, steps, step, 0)

    total = jnp.sum(ssq_s[...], axis=1, keepdims=True) * (1.0 / (heads * D))
    ssq_s[...] = jnp.broadcast_to(lax.rsqrt(total + EPS), (tok, D))

    for s in range(hn // g):
        h0 = me * hn + s * g
        pos = h0 % hc
        src = (planes - 1) * GROUP + ((pos % half) // w) * 2 + pos // half

        @pl.when(src != me)
        def _():
            send(
                s_out.at[0, pl.ds(0, g)], fin_s.at[pl.ds(s * g, g)], f_ss.at[0, 0], f_rs.at[s], core_peer
            ).wait_recv()

    for d in range(1, GROUP):
        fac_copy(d).wait_send()

    def drain(j, carry):
        core_copy(j).wait_send()
        pair_copy(j).wait_send()
        e_copy(j).wait_send()
        x_copy(j).wait_send()
        store(j).wait()

        @pl.when(plane < planes - 1)
        def _():
            z_copy(j).wait_send()

        @pl.when(plane == planes - 1)
        def _():
            for s in range(w // g):
                dev, _off = fin_place(j, s)

                @pl.when(dev != me)
                def _():
                    fin_copy(j, s).wait_send()

        return carry

    lax.fori_loop(0, chunks, drain, 0)


def finish_kernel(mix_ref, inv_ref, fin_in, out_ref, fin_ref):
    inv = inv_ref[...]
    for t in range(mix_ref.shape[1] // D):
        at = slice(t * D, (t + 1) * D)
        out_ref[:, at] = (mix_ref[:, at].astype(F32) * inv).astype(BF16)
    fin_ref[...] = fin_in[...].astype(F32)


def shards(n, queries, keys_in, values_in, log_decay, gate_logits, norm_gain, doc_lengths):
    tok, width = queries.shape
    heads = width // D
    chunks = CHUNKS
    hc = heads // chunks
    half = hc // 2
    w = half // 2
    hn = heads // n
    g = math.gcd(w, hn)
    vm = pltpu.VMEM
    dma = pltpu.SemaphoreType.DMA
    anyspace = pl.BlockSpec(memory_space=pl.ANY)
    vspec = pl.BlockSpec(memory_space=pltpu.VMEM)
    part = vm((chunks, w, D, D), BF16)
    scratch = [
        vm((tok, width), F32),
        vm((tok, width), BF16), vm((tok, width), BF16), vm((tok, width), BF16), vm((tok, width), BF16),
        vm((tok, tok), F32),
        vm((heads, tok), F32), vm((2 * chunks, tok, half), F32), vm((chunks, tok, 2 * hc), F32),
        vm((heads, D), F32), vm((GROUP, heads, D), F32),
        vm((chunks, 2, 2, w, D, D), BF16), vm((chunks, 2, w, D, D), BF16), vm((chunks, w, D, D), F32),
        part, part, part, part, part,
        vm((chunks, 2, w, D, D), BF16), vm((chunks, 2, w, D, D), BF16),
        vm((chunks, 2, 2, w, D, D), BF16),
        dma((4, chunks)), dma((chunks,)), dma((GROUP - 1,)), dma((GROUP - 1,)),
        dma((chunks,)), dma((chunks,)), dma((chunks,)), dma((chunks,)), dma((chunks,)), dma((chunks,)),
        dma((chunks,)), dma((chunks,)), dma((chunks,)), dma((chunks,)),
        dma((chunks, w // g)), dma((hn // g,)), dma,
    ]
    mixed, squares, final = pl.pallas_call(
        functools.partial(kernel, n, heads, chunks),
        out_shape=(
            jax.ShapeDtypeStruct((tok, width), BF16),
            jax.ShapeDtypeStruct((tok, D), F32),
            jax.ShapeDtypeStruct((hn, D, D), BF16),
        ),
        in_specs=[anyspace] * 4 + [vspec, vspec, pl.BlockSpec(memory_space=pltpu.SMEM)],
        out_specs=(anyspace, vspec, vspec),
        scratch_shapes=scratch,
        compiler_params=pltpu.CompilerParams(
            collective_id=0, has_side_effects=True, vmem_limit_bytes=60 * 1024 * 1024
        ),
    )(queries, keys_in, values_in, gate_logits, log_decay.T, norm_gain.reshape(1, width), doc_lengths)
    rows = tok // FINISH_PARTS
    return pl.pallas_call(
        finish_kernel,
        out_shape=(
            jax.ShapeDtypeStruct((tok, width), BF16),
            jax.ShapeDtypeStruct((hn, D, D), F32),
        ),
        grid=(FINISH_PARTS,),
        in_specs=[
            pl.BlockSpec((rows, width), lambda i: (i, 0)),
            pl.BlockSpec((rows, D), lambda i: (i, 0)),
            pl.BlockSpec((hn, D, D), lambda i: (0, 0, 0)),
        ],
        out_specs=(
            pl.BlockSpec((rows, width), lambda i: (i, 0)),
            pl.BlockSpec((hn, D, D), lambda i: (0, 0, 0)),
        ),
        compiler_params=pltpu.CompilerParams(vmem_limit_bytes=60 * 1024 * 1024),
    )(mixed, squares, final)


def solution(mesh):
    rows = P(("grp", "seq"), None)
    return jax.shard_map(
        functools.partial(shards, mesh.shape["seq"]),
        mesh=mesh,
        in_specs=(rows, rows, rows, rows, rows, P(), P("grp")),
        out_specs=(rows, P(("grp", "seq"), None, None)),
        check_vma=False,
    )
```

profile of v0, /device:TPU:25, one launch (start us, length us, event | category | flops | bytes accessed | tf_op | source)
XLA Modules:
  0.0 49.2 jit_solution(567439996977301341)
XLA Ops:
  0.6 44.3 %shard_map.86 = (bf16[256,8192]{1,0:T(8,128)(2,1)}, f32[256,128]{1,0:T(8,128)}, bf16[4,128,128]{2,1,0:T(8,128)(2,1)}) custom-call(bf16[256,8192]{1,0:T(8,128)(2,1)} %q_hbm.1, bf16[256,8192]{1,0:T(8,128)(2,1)} %k_hbm.1, bf16[256,8192]{1,0:T(8,128)(2,1)} %v_hbm.1, bf16[256,8192]{1,0:T(8,128)(2,1)} %g_hbm.1, bf16[64,256]{1,0:T(8,128)(2,1)} %bitcast.2, ...), custom_call_target="tpu_custom_call" | custom-call | tf_op jit(solution)/shard_map/pallas_call | solution.py:404
  45.0 4.2 %shard_map.87 = (bf16[256,8192]{1,0:T(8,128)(2,1)}, f32[4,128,128]{2,1,0:T(8,128)}) custom-call(bf16[256,8192]{1,0:T(8,128)(2,1)} %get-tuple-element.5.mix_ref, f32[256,128]{1,0:T(8,128)} %get-tuple-element.6.inv_ref, bf16[4,128,128]{2,1,0:T(8,128)(2,1)} %get-tuple-element.7.fin_in), custom_call_target="tpu_custom_call" | custom-call | tf_op jit(solution)/shard_map/pallas_call | solution.py:419
where the time goes:
time: 49.5 us; the launch traced here: 49.2 us
  Pallas kernels  48.6 us (98%)
  between operations  0.64 us (1%)
    pallas_call x1, Pallas kernels, shards(): pl.pallas_call(functools.partial(kernel, n, heads, chunks), out_shape=(ja...  44.3 us
    pallas_call x1, Pallas kernels, shards(): pl.pallas_call(finish_kernel, out_shape=(jax.ShapeDtypeStruct((tok, width...  4.21 us

commit v1 on v0

v1 whole, which is shorter than its diff:
```python
import functools
import math

import jax
import jax.numpy as jnp
from jax import lax
from jax.experimental import pallas as pl
from jax.experimental.pallas import tpu as pltpu
from jax.sharding import PartitionSpec as P

EPS = 1e-05
LOG2E = 1.4426950408889634
D = 128
GROUP = 4
CHUNKS = 8
CHAIN_LAG = 4
HOP_LAG = 2
E_LAG = 4
X_LAG = 2
FINISH_PARTS = 8
F32, BF16 = jnp.float32, jnp.bfloat16
MESH = pl.DeviceIdType.MESH


def dot(a, b, dims):
    return lax.dot_general(a, b, (dims, ((), ())), preferred_element_type=F32)


def kernel(
    n, heads, chunks,
    q_hbm, k_hbm, v_hbm, g_hbm, ld_hbm, gain_hbm, docs_hbm,
    out_s, ssq_s, fin_s,
    mix_s, gate_s, q_s, k_s, v_s, g_s, kt_s, ld_s, gain_s, docs_s, pen_s, cumt_s, kwt_s, cum_s, lead_s,
    fac_own, fac_core, fac_chip, fac_pair, u_own, u_core, u_mine, u_send, u_pair, s_in, s_out, e_send, e_half,
    x_send, ent,
    load_sem, small_sem, fac_ss, fac_rs, core_ss, core_rs, pair_ss, pair_rs, z_ss, z_rs, e_ss, e_rs,
    x_ss, x_rs, f_ss, f_rs, f_ls,
):
    tok = q_hbm.shape[0]
    hc = heads // chunks
    half = hc // 2
    w = half // 2
    planes = n // GROUP
    hn = heads // n
    g = math.gcd(w, hn)
    span = 2 * hn
    m = span // half
    me = lax.axis_index("seq")
    plane = me // GROUP
    r = me % GROUP
    y = r // 2
    c = r % 2
    core_peer = plane * GROUP + y * 2 + (1 - c)
    pair_peer = plane * GROUP + (1 - y) * 2 + c

    def send(src, dst, ss, rs, dev):
        return pltpu.make_async_remote_copy(
            src_ref=src, dst_ref=dst, send_sem=ss, recv_sem=rs,
            device_id={"seq": dev}, device_id_type=MESH,
        )

    def head0(j, yh):
        return (j // m) * (2 * span) + yh * span + (j % m) * half

    def hcols(j, yh):
        return pl.ds(pl.multiple_of(head0(j, yh) * D, half * D), half * D)

    def hcol(j, yh, hh):
        return pl.ds(pl.multiple_of((head0(j, yh) + hh) * D, D), D)

    def load(which, hbm, vm, j, yh):
        at = hcols(j, yh)
        return pltpu.make_async_copy(hbm.at[:, at], vm.at[:, at], load_sem.at[which, j, yh])

    def start_pair(a, a_hbm, a_vm, b, b_hbm, b_vm):
        def go(j, carry):
            for yh in range(2):
                load(a, a_hbm, a_vm, j, yh).start()
                load(b, b_hbm, b_vm, j, yh).start()
            return carry
        return go

    ld_copy = pltpu.make_async_copy(ld_hbm, ld_s.at[pl.ds(0, heads)], small_sem.at[0])
    docs_copy = pltpu.make_async_copy(docs_hbm, docs_s, small_sem.at[1])
    gain_copy = pltpu.make_async_copy(gain_hbm, gain_s, small_sem.at[2])
    ld_copy.start()
    docs_copy.start()
    lax.fori_loop(0, chunks, start_pair(0, k_hbm, k_s, 1, v_hbm, v_s), 0)

    barrier = pltpu.get_barrier_semaphore()
    for d in range(1, GROUP):
        pl.semaphore_signal(
            barrier, inc=1, device_id={"seq": plane * GROUP + (r + d) % GROUP}, device_id_type=MESH
        )

    @pl.when(plane > 0)
    def _():
        pl.semaphore_signal(barrier, inc=1, device_id={"seq": me - GROUP}, device_id_type=MESH)

    gain_copy.start()
    lax.fori_loop(0, chunks, start_pair(2, q_hbm, q_s, 3, g_hbm, g_s), 0)

    if heads < D:
        ld_s[pl.ds(heads, D - heads)] = jnp.zeros((D - heads, tok), BF16)
    base = me * tok
    row_i = lax.broadcasted_iota(jnp.int32, (tok, tok), 0)
    col_i = lax.broadcasted_iota(jnp.int32, (tok, tok), 1)
    causal = row_i >= col_i
    lanes = lax.broadcasted_iota(jnp.int32, (1, tok), 1)
    docs_copy.wait()
    n_docs = docs_s.shape[0]
    doc_row = jnp.zeros((1, tok), jnp.int32)
    before = jnp.int32(0)
    last = jnp.int32(0)
    end = jnp.int32(0)
    for d in range(n_docs):
        end = end + docs_s[d]
        doc_row = doc_row + jnp.where(lanes + base >= end, 1, 0)
        before = before + jnp.where(base - 1 >= end, 1, 0)
        last = last + jnp.where(base + tok - 1 >= end, 1, 0)
    closing = jnp.where(doc_row == last, 1.0, 0.0).astype(F32)
    ld_copy.wait()
    upper = jnp.where(row_i <= col_i, 1.0, 0.0).astype(BF16)
    cumt = dot(ld_s[pl.ds(0, heads)], upper, ((1,), (0,)))
    cumt_s[...] = LOG2E * cumt
    total = cumt[:, tok - 1:tok]
    kwt_s[...] = closing * jnp.exp(total - cumt)

    def updates(j):
        for yh in range(2):
            load(0, k_hbm, k_s, j, yh).wait()
            load(1, v_hbm, v_s, j, yh).wait()

    def update_math(j):
        for yh in range(2):
            for hh in range(half):
                h = head0(j, yh) + hh
                kt = k_s[:, hcol(j, yh, hh)].T
                kt_s[h] = kt
                wk = (kt.astype(F32) * kwt_s[pl.ds(h, 1), :]).astype(BF16)
                up = dot(wk, v_s[:, hcol(j, yh, hh)], ((1,), (0,)))
                u_own[j, hh // w, yh, hh % w] = up.astype(BF16)

    def core_copy(j):
        return send(u_own.at[j, 1 - c], u_core.at[j], core_ss.at[j], core_rs.at[j], core_peer)

    def pair_copy(j):
        return send(u_send.at[j], u_pair.at[j], pair_ss.at[j], pair_rs.at[j], pair_peer)

    def z_copy(j):
        return send(s_out.at[j], s_in.at[j], z_ss.at[j], z_rs.at[j], (me + GROUP) % n)

    def e_copy(j):
        return send(e_send.at[j], e_half.at[j, y], e_ss.at[j], e_rs.at[j], pair_peer)

    def x_copy(j):
        return send(x_send.at[j], ent.at[j, c], x_ss.at[j], x_rs.at[j], core_peer)

    def fac_core_copy():
        return send(fac_own, fac_core, fac_ss.at[0], fac_rs.at[0], core_peer)

    def fac_pair_copy():
        return send(fac_chip.at[c, 1 - y], fac_pair, fac_ss.at[1], fac_rs.at[1], pair_peer)

    def combine(j):
        core_copy(j).wait_recv()
        for k in range(w):
            for yo in range(2):
                at = pl.ds(j * w + k, 1)
                fa = jnp.where(c == 0, fac_core[c, yo, at, :], 1.0)
                fb = jnp.where(c == 0, 1.0, fac_own[c, yo, at, :])
                val = fa * u_own[j, c, yo, k].astype(F32) + fb * u_core[j, yo, k].astype(F32)

                @pl.when(yo == y)
                def _():
                    u_mine[j, k] = val

                @pl.when(yo != y)
                def _():
                    u_send[j, k] = val.astype(BF16)
        pair_copy(j).start()

    def fin_place(j, s):
        h = head0(j, y) + c * w + s * g
        return h // hn, h % hn

    def fin_copy(j, s):
        dev, off = fin_place(j, s)
        return send(
            s_out.at[j, pl.ds(s * g, g)], fin_s.at[pl.ds(off, g)],
            f_ss.at[j, s], f_rs.at[off // g], dev,
        )

    def fin_local(j, s):
        _, off = fin_place(j, s)
        return pltpu.make_async_copy(s_out.at[j, pl.ds(s * g, g)], fin_s.at[pl.ds(off, g)], f_ls)

    def chain(j):
        pair_copy(j).wait_recv()

        @pl.when(plane > 0)
        def _():
            z_copy(j).wait_recv()

        for k in range(w):
            at = pl.ds(j * w + k, 1)
            chip = fac_chip[c, y, at, :]
            other_chip = fac_pair[at, :]
            f01 = jnp.where(y == 0, chip, other_chip)
            f23 = jnp.where(y == 0, other_chip, chip)
            mine = u_mine[j, k]
            other = u_pair[j, k].astype(F32)
            entry = s_in[j, k].astype(F32)
            mid = f01 * entry + jnp.where(y == 0, mine, other)
            s_out[j, k] = (f23 * mid + jnp.where(y == 0, other, mine)).astype(BF16)
            e_send[j, k] = jnp.where(y == 0, mid, entry).astype(BF16)
            e_half[j, y, k] = jnp.where(y == 0, entry, mid).astype(BF16)

        @pl.when(plane < planes - 1)
        def _():
            z_copy(j).start()

        @pl.when(plane == planes - 1)
        def _():
            for s in range(w // g):
                dev, _off = fin_place(j, s)

                @pl.when(dev != me)
                def _():
                    fin_copy(j, s).start()

                @pl.when(dev == me)
                def _():
                    fin_local(j, s).start()
                    fin_local(j, s).wait()

    def inside_wait(i):
        load(2, q_hbm, q_s, i // 2, i % 2).wait()
        load(3, g_hbm, g_s, i // 2, i % 2).wait()

    def inside(i):
        j = i // 2
        yh = i % 2
        h0 = head0(j, yh)
        blk = tok // 2
        cols = pltpu.roll(cum_s[...], (D - h0) % D, 1)
        for hh in range(half):
            at = hcol(j, yh, hh)
            row = cumt_s[pl.ds(h0 + hh, 1), :]
            kt = kt_s[h0 + hh]
            ci = cols[:, hh:hh + 1]
            top = dot(q_s[:blk, at], kt[:, :blk], ((1,), (0,)))
            bot = dot(q_s[blk:, at], kt, ((1,), (0,)))
            top = (top * jnp.exp2((ci[:blk] - row[:, :blk]) + pen_s[:blk, :blk])).astype(BF16)
            bot = (bot * jnp.exp2((ci[blk:] - row) + pen_s[blk:, :])).astype(BF16)
            top = jnp.concatenate([top, jnp.zeros_like(top)], axis=1)
            wt = jnp.concatenate([top, bot], axis=0)
            mix_s[:, at] = dot(wt, v_s[:, at], ((1,), (0,)))
            hg = 0.5 * gain_s[:, at]
            gate_s[:, at] = hg * jnp.tanh(0.5 * g_s[:, at].astype(F32)) + hg

    def spread(j):
        e_copy(j).wait_recv()
        for yo in range(2):
            for k in range(w):
                at = pl.ds(j * w + k, 1)
                f0 = jnp.where(c == 0, fac_own[c, yo, at, :], fac_core[c, yo, at, :])
                first = e_half[j, yo, k]
                u0 = jnp.where(c == 0, u_own[j, 0, yo, k], u_core[j, yo, k]).astype(F32)
                second = (f0 * first.astype(F32) + u0).astype(BF16)
                ent[j, c, yo, k] = jnp.where(c == 0, first, second)
                x_send[j, yo, k] = jnp.where(c == 0, second, first)
        x_copy(j).start()

    def across(j):
        core_copy(j).wait_send()
        pair_copy(j).wait_send()
        e_copy(j).wait_send()

        @pl.when(plane < planes - 1)
        def _():
            z_copy(j).wait_send()

        @pl.when(plane == planes - 1)
        def _():
            for s in range(w // g):
                dev, _off = fin_place(j, s)

                @pl.when(dev != me)
                def _():
                    fin_copy(j, s).wait_send()

        x_copy(j).wait_recv()
        x_copy(j).wait_send()
        cols = pltpu.roll(lead_s[...], (D - head0(j, 0)) % D, 1)
        for yh in range(2):
            acc = ssq_s[...]
            for hh in range(half):
                at = hcol(j, yh, hh)
                lane = yh * span + hh
                st = ent[j, hh // w, yh, hh % w]
                mixed = mix_s[:, at] + cols[:, lane:lane + 1] * dot(q_s[:, at], st, ((1,), (0,)))
                acc = acc + mixed * mixed
                out_s[:, at] = (mixed * gate_s[:, at]).astype(BF16)
            ssq_s[...] = acc

    updates(0)
    update_math(0)
    own_f = jnp.where(last == before, 1.0, 0.0).astype(F32) * jnp.exp(jnp.broadcast_to(total, (heads, D)))
    for j in range(chunks):
        for yh in range(2):
            for cc in range(2):
                h = head0(j, yh) + cc * w
                fac_own[cc, yh, j * w:(j + 1) * w, :] = own_f[h:h + w]

    @pl.when(plane < planes - 1)
    def _():
        pl.semaphore_wait(barrier, GROUP)

    @pl.when(plane == planes - 1)
    def _():
        pl.semaphore_wait(barrier, GROUP - 1)

    core_copy(0).start()
    fac_core_copy().start()
    updates(1)
    update_math(1)
    core_copy(1).start()
    fac_core_copy().wait_recv()
    combine(0)
    fac_chip[...] = fac_own[...] * fac_core[...]
    fac_pair_copy().start()

    rows = lax.broadcasted_iota(jnp.int32, (tok, D), 0)
    doc_col = jnp.zeros((tok, D), jnp.int32)
    end = jnp.int32(0)
    for d in range(n_docs):
        end = end + docs_s[d]
        doc_col = doc_col + jnp.where(rows + base >= end, 1, 0)
    pen_s[...] = jnp.where(causal & (doc_col[:, :1] == doc_row), 0.0, -1e30).astype(F32)
    tri = jnp.where(causal, 1.0, 0.0).astype(BF16)
    cum = dot(tri, ld_s[...], ((1,), (1,)))
    cum_s[...] = LOG2E * cum
    lead_s[...] = jnp.where(doc_col == before, 1.0, 0.0).astype(F32) * jnp.exp(cum)
    ssq_s[...] = jnp.zeros_like(ssq_s)

    @pl.when(plane == 0)
    def _():
        s_in[...] = jnp.zeros_like(s_in)

    gain_copy.wait()
    fac_pair_copy().wait_recv()

    chain_lag = CHAIN_LAG + HOP_LAG * plane
    e_lag = jnp.maximum(chain_lag, chunks)
    spread_lag = e_lag + E_LAG
    across_lag = spread_lag + X_LAG
    steps = jnp.maximum(chunks + across_lag, 2 * chunks + 2)

    def step(t, carry):
        def at(lag, count, body):
            @pl.when((t >= lag) & (t < lag + count))
            def _():
                body(t - lag)

        at(1, chunks, combine)
        at(chain_lag, chunks, chain)
        at(e_lag, chunks, lambda j: e_copy(j).start())
        at(spread_lag, chunks, spread)

        @pl.when(t < chunks)
        def _():
            updates(t)
            inside_wait(t - 2)
            update_math(t)
            inside(t - 2)
            core_copy(t).start()

        @pl.when((t >= chunks) & (t < 2 * chunks + 2))
        def _():
            inside_wait(t - 2)
            inside(t - 2)

        at(across_lag, chunks, across)
        return carry

    lax.fori_loop(2, steps, step, 0)

    mean = jnp.sum(ssq_s[...], axis=1, keepdims=True) * (1.0 / (heads * D))
    ssq_s[...] = jnp.broadcast_to(lax.rsqrt(mean + EPS), (tok, D))

    for s in range(hn // g):
        h = me * hn + s * g
        src = (planes - 1) * GROUP + ((h // span) % 2) * 2 + (h % half) // w

        @pl.when(src != me)
        def _():
            send(
                s_out.at[0, pl.ds(0, g)], fin_s.at[pl.ds(s * g, g)], f_ss.at[0, 0], f_rs.at[s], core_peer
            ).wait_recv()

    fac_core_copy().wait_send()
    fac_pair_copy().wait_send()


def finish_kernel(mix_ref, inv_ref, fin_in, out_hbm, fin_ref, buf, sem):
    parts = buf.shape[0]
    rows = buf.shape[1]
    copies = []
    for p in range(parts):
        at = slice(p * rows, (p + 1) * rows)
        inv = inv_ref[at, :]
        for t in range(mix_ref.shape[1] // D):
            cols = slice(t * D, (t + 1) * D)
            buf[p, :, cols] = (mix_ref[at, cols].astype(F32) * inv).astype(BF16)
        copy = pltpu.make_async_copy(buf.at[p], out_hbm.at[pl.ds(p * rows, rows)], sem.at[p])
        copy.start()
        copies.append(copy)
    fin_ref[...] = fin_in[...].astype(F32)
    for copy in copies:
        copy.wait()


def shards(n, queries, keys_in, values_in, log_decay, gate_logits, norm_gain, doc_lengths):
    tok, width = queries.shape
    heads = width // D
    chunks = CHUNKS
    hc = heads // chunks
    half = hc // 2
    w = half // 2
    hn = heads // n
    g = math.gcd(w, hn)
    vm = pltpu.VMEM
    dma = pltpu.SemaphoreType.DMA
    anyspace = pl.BlockSpec(memory_space=pl.ANY)
    vspec = pl.BlockSpec(memory_space=pltpu.VMEM)
    part = vm((chunks, w, D, D), BF16)
    fac = vm((2, 2, chunks * w, D), F32)
    scratch = [
        vm((tok, width), F32), vm((tok, width), F32),
        vm((tok, width), BF16), vm((tok, width), BF16), vm((tok, width), BF16), vm((tok, width), BF16),
        vm((heads, D, tok), BF16), vm((max(heads, D), tok), BF16), vm((1, width), F32),
        pltpu.SMEM(doc_lengths.shape, jnp.int32),
        vm((tok, tok), F32), vm((heads, tok), F32), vm((heads, tok), F32), vm((tok, D), F32), vm((tok, D), F32),
        fac, fac, fac, vm((chunks * w, D), F32),
        vm((chunks, 2, 2, w, D, D), BF16), vm((chunks, 2, w, D, D), BF16), vm((chunks, w, D, D), F32),
        part, part, part, part, part,
        vm((chunks, 2, w, D, D), BF16), vm((chunks, 2, w, D, D), BF16),
        vm((chunks, 2, 2, w, D, D), BF16),
        dma((4, chunks, 2)), dma((3,)), dma((2,)), dma((2,)),
        dma((chunks,)), dma((chunks,)), dma((chunks,)), dma((chunks,)), dma((chunks,)), dma((chunks,)),
        dma((chunks,)), dma((chunks,)), dma((chunks,)), dma((chunks,)),
        dma((chunks, w // g)), dma((hn // g,)), dma,
    ]
    mixed, squares, final = pl.pallas_call(
        functools.partial(kernel, n, heads, chunks),
        out_shape=(
            pltpu.VMEM((tok, width), BF16),
            pltpu.VMEM((tok, D), F32),
            pltpu.VMEM((hn, D, D), BF16),
        ),
        in_specs=[anyspace] * 7,
        out_specs=(vspec, vspec, vspec),
        scratch_shapes=scratch,
        compiler_params=pltpu.CompilerParams(
            collective_id=0, has_side_effects=True, vmem_limit_bytes=54 * 1024 * 1024
        ),
    )(queries, keys_in, values_in, gate_logits, log_decay.T, norm_gain.reshape(1, width), doc_lengths)
    rows = tok // FINISH_PARTS
    return pl.pallas_call(
        finish_kernel,
        out_shape=(
            jax.ShapeDtypeStruct((tok, width), BF16),
            jax.ShapeDtypeStruct((hn, D, D), F32),
        ),
        in_specs=[vspec, vspec, vspec],
        out_specs=(anyspace, vspec),
        scratch_shapes=[vm((FINISH_PARTS, rows, width), BF16), dma((FINISH_PARTS,))],
        compiler_params=pltpu.CompilerParams(vmem_limit_bytes=16 * 1024 * 1024),
    )(mixed, squares, final)


def solution(mesh):
    rows = P(("grp", "seq"), None)
    return jax.shard_map(
        functools.partial(shards, mesh.shape["seq"]),
        mesh=mesh,
        in_specs=(rows, rows, rows, rows, rows, P(), P("grp")),
        out_specs=(rows, P(("grp", "seq"), None, None)),
        check_vma=False,
    )
```

time: 49.5 us -> 45.9 us (0.927)
  Pallas kernels: 48.6 us -> 45.1 us
    pallas_call x1, Pallas kernels: 44.3 us -> 42.2 us  [shards(): pl.pallas_call(functools.partial(kernel, n, heads, chunks), out_shape=(pl...]
    pallas_call x1, Pallas kernels: 4.21 us -> 2.88 us  [shards(): pl.pallas_call(finish_kernel, out_shape=(jax.ShapeDtypeStruct((tok, width...]
where the time goes in v1:
time: 45.9 us; the launch traced here: 45.7 us
  Pallas kernels  45.1 us (98%)
  between operations  0.64 us (1%)
    pallas_call x1, Pallas kernels, shards(): pl.pallas_call(functools.partial(kernel, n, heads, chunks), out_shape=(pl...  42.2 us
    pallas_call x1, Pallas kernels, shards(): pl.pallas_call(finish_kernel, out_shape=(jax.ShapeDtypeStruct((tok, width...  2.88 us

profile of v1, /device:TPU:25, one launch (start us, length us, event | category | flops | bytes accessed | tf_op | source)
XLA Modules:
  0.0 45.7 jit_solution(14180380368518724277)
XLA Ops:
  0.6 42.2 %shard_map.86 = (bf16[256,8192]{1,0:T(8,128)(2,1)S(1)}, f32[256,128]{1,0:T(8,128)S(1)}, bf16[4,128,128]{2,1,0:T(8,128)(2,1)S(1)}) custom-call(bf16[256,8192]{1,0:T(8,128)(2,1)} %q_hbm.1, bf16[256,8192]{1,0:T(8,128)(2,1)} %k_hbm.1, bf16[256,8192]{1,0:T(8,128)(2,1)} %v_hbm.1, bf16[256,8192]{1,0:T(8,128)(2,1)} %g_hbm.1, bf16[64,256]{1,0:T(8,128)(2,1)} %bitcast.2, ...), custom_call_target="tpu_custom_call" | custom-call | tf_op jit(solution)/shard_map/pallas_call | solution.py:455
  42.8 2.9 %shard_map.87 = (bf16[256,8192]{1,0:T(8,128)(2,1)}, f32[4,128,128]{2,1,0:T(8,128)}) custom-call(bf16[256,8192]{1,0:T(8,128)(2,1)S(1)} %get-tuple-element.5.mix_ref, f32[256,128]{1,0:T(8,128)S(1)} %get-tuple-element.6.inv_ref, bf16[4,128,128]{2,1,0:T(8,128)(2,1)S(1)} %get-tuple-element.7.fin_in), custom_call_target="tpu_custom_call" | custom-call | tf_op jit(solution)/shard_map/pallas_call | solution.py:470

commit v2 on v1

--- a/solution.py
+++ b/solution.py
@@ -196,6 +196,10 @@
         return pltpu.make_async_copy(s_out.at[j, pl.ds(s * g, g)], fin_s.at[pl.ds(off, g)], f_ls)
 
     def chain(j):
+        @pl.when(j == 0)
+        def _():
+            fac_pair_copy().wait_recv()
+
         pair_copy(j).wait_recv()
 
         @pl.when(plane > 0)
@@ -326,11 +330,6 @@
     updates(1)
     update_math(1)
     core_copy(1).start()
-    fac_core_copy().wait_recv()
-    combine(0)
-    fac_chip[...] = fac_own[...] * fac_core[...]
-    fac_pair_copy().start()
-
     rows = lax.broadcasted_iota(jnp.int32, (tok, D), 0)
     doc_col = jnp.zeros((tok, D), jnp.int32)
     end = jnp.int32(0)
@@ -349,10 +348,12 @@
         s_in[...] = jnp.zeros_like(s_in)
 
     gain_copy.wait()
-    fac_pair_copy().wait_recv()
+    fac_core_copy().wait_recv()
+    fac_chip[...] = fac_own[...] * fac_core[...]
+    fac_pair_copy().start()
 
     chain_lag = CHAIN_LAG + HOP_LAG * plane
-    e_lag = jnp.maximum(chain_lag, chunks)
+    e_lag = jnp.maximum(chain_lag, chunks + 2)
     spread_lag = e_lag + E_LAG
     across_lag = spread_lag + X_LAG
     steps = jnp.maximum(chunks + across_lag, 2 * chunks + 2)
@@ -363,7 +364,7 @@
             def _():
                 body(t - lag)
 
-        at(1, chunks, combine)
+        at(2, chunks, combine)
         at(chain_lag, chunks, chain)
         at(e_lag, chunks, lambda j: e_copy(j).start())
         at(spread_lag, chunks, spread)

time: 45.9 us -> 38.5 us (0.84)
  Pallas kernels: 45.1 us -> 37.7 us
    pallas_call x1, Pallas kernels: 42.2 us -> 34.9 us  [shards(): pl.pallas_call(functools.partial(kernel, n, heads, chunks), out_shape=(pl...]
where the time goes in v2:
time: 38.5 us; the launch traced here: 38.4 us
  Pallas kernels  37.7 us (98%)
  between operations  0.64 us (2%)
    pallas_call x1, Pallas kernels, shards(): pl.pallas_call(functools.partial(kernel, n, heads, chunks), out_shape=(pl...  34.9 us
    pallas_call x1, Pallas kernels, shards(): pl.pallas_call(finish_kernel, out_shape=(jax.ShapeDtypeStruct((tok, width...  2.88 us

profile of v2, /device:TPU:25, one launch (start us, length us, event | category | flops | bytes accessed | tf_op | source)
XLA Modules:
  0.0 38.4 jit_solution(11946550625419870530)
XLA Ops:
  0.6 34.9 %shard_map.86 = (bf16[256,8192]{1,0:T(8,128)(2,1)S(1)}, f32[256,128]{1,0:T(8,128)S(1)}, bf16[4,128,128]{2,1,0:T(8,128)(2,1)S(1)}) custom-call(bf16[256,8192]{1,0:T(8,128)(2,1)} %q_hbm.1, bf16[256,8192]{1,0:T(8,128)(2,1)} %k_hbm.1, bf16[256,8192]{1,0:T(8,128)(2,1)} %v_hbm.1, bf16[256,8192]{1,0:T(8,128)(2,1)} %g_hbm.1, bf16[64,256]{1,0:T(8,128)(2,1)} %bitcast.2, ...), custom_call_target="tpu_custom_call" | custom-call | tf_op jit(solution)/shard_map/pallas_call | solution.py:456
  35.5 2.9 %shard_map.87 = (bf16[256,8192]{1,0:T(8,128)(2,1)}, f32[4,128,128]{2,1,0:T(8,128)}) custom-call(bf16[256,8192]{1,0:T(8,128)(2,1)S(1)} %get-tuple-element.5.mix_ref, f32[256,128]{1,0:T(8,128)S(1)} %get-tuple-element.6.inv_ref, bf16[4,128,128]{2,1,0:T(8,128)(2,1)S(1)} %get-tuple-element.7.fin_in), custom_call_target="tpu_custom_call" | custom-call | tf_op jit(solution)/shard_map/pallas_call | solution.py:471

commit v3 on v1

--- a/solution.py
+++ b/solution.py
@@ -12,10 +12,11 @@
 LOG2E = 1.4426950408889634
 D = 128
 GROUP = 4
-CHUNKS = 8
-CHAIN_LAG = 4
-HOP_LAG = 2
-E_LAG = 4
+CHUNKS = 16
+LOADS = 8
+CHAIN_LAG = 9
+HOP_LAG = 4
+E_LAG = 5
 X_LAG = 2
 FINISH_PARTS = 8
 F32, BF16 = jnp.float32, jnp.bfloat16
@@ -30,10 +31,10 @@
     n, heads, chunks,
     q_hbm, k_hbm, v_hbm, g_hbm, ld_hbm, gain_hbm, docs_hbm,
     out_s, ssq_s, fin_s,
-    mix_s, gate_s, q_s, k_s, v_s, g_s, kt_s, ld_s, gain_s, docs_s, pen_s, cumt_s, kwt_s, cum_s, lead_s,
-    fac_own, fac_core, fac_chip, fac_pair, u_own, u_core, u_mine, u_send, u_pair, s_in, s_out, e_send, e_half,
+    mix_s, gate_s, kv_s, qg_s, kt_s, ld_s, gain_s, docs_s, pen_s, cumt_s, kwt_s, cum_s, lead_s,
+    fac_own, fac_core, fac_chip, fac_pair, wt_s, u_own, u_core, u_mine, u_send, u_pair, s_in, s_out, e_send, e_half,
     x_send, ent,
-    load_sem, small_sem, fac_ss, fac_rs, core_ss, core_rs, pair_ss, pair_rs, z_ss, z_rs, e_ss, e_rs,
+    kv_sem, qg_sem, small_sem, fac_ss, fac_rs, core_ss, core_rs, pair_ss, pair_rs, z_ss, z_rs, e_ss, e_rs,
     x_ss, x_rs, f_ss, f_rs, f_ls,
 ):
     tok = q_hbm.shape[0]
@@ -41,6 +42,8 @@
     half = hc // 2
     w = half // 2
     planes = n // GROUP
+    loads = LOADS
+    per = chunks // loads
     hn = heads // n
     g = math.gcd(w, hn)
     span = 2 * hn
@@ -62,43 +65,44 @@
     def head0(j, yh):
         return (j // m) * (2 * span) + yh * span + (j % m) * half
 
-    def hcols(j, yh):
-        return pl.ds(pl.multiple_of(head0(j, yh) * D, half * D), half * D)
-
     def hcol(j, yh, hh):
         return pl.ds(pl.multiple_of((head0(j, yh) + hh) * D, D), D)
 
-    def load(which, hbm, vm, j, yh):
-        at = hcols(j, yh)
-        return pltpu.make_async_copy(hbm.at[:, at], vm.at[:, at], load_sem.at[which, j, yh])
-
-    def start_pair(a, a_hbm, a_vm, b, b_hbm, b_vm):
-        def go(j, carry):
+    k_s, v_s = kv_s.at[0], kv_s.at[1]
+    q_s, g_s = qg_s.at[0], qg_s.at[1]
+
+    def fetch(first, second, both, sem):
+        def go(p, carry):
             for yh in range(2):
-                load(a, a_hbm, a_vm, j, yh).start()
-                load(b, b_hbm, b_vm, j, yh).start()
+                at = pl.ds(pl.multiple_of(head0(p * per, yh) * D, half * per * D), half * per * D)
+                pltpu.make_async_copy(first.at[:, at], both.at[0, :, at], sem.at[p]).start()
+                pltpu.make_async_copy(second.at[:, at], both.at[1, :, at], sem.at[p]).start()
             return carry
         return go
+
+    def fetched(both, sem, p):
+        part = both.at[:, :, pl.ds(0, 2 * half * per * D)]
+        pltpu.make_async_copy(part, part, sem.at[p]).wait()
+
+    barrier = pltpu.get_barrier_semaphore()
+    for d in range(1, GROUP):
+        pl.semaphore_signal(
+            barrier, inc=1, device_id={"seq": plane * GROUP + (r + d) % GROUP}, device_id_type=MESH
+        )
+
+    @pl.when(plane > 0)
+    def _():
+        pl.semaphore_signal(barrier, inc=1, device_id={"seq": me - GROUP}, device_id_type=MESH)
 
     ld_copy = pltpu.make_async_copy(ld_hbm, ld_s.at[pl.ds(0, heads)], small_sem.at[0])
     docs_copy = pltpu.make_async_copy(docs_hbm, docs_s, small_sem.at[1])
     gain_copy = pltpu.make_async_copy(gain_hbm, gain_s, small_sem.at[2])
     ld_copy.start()
     docs_copy.start()
-    lax.fori_loop(0, chunks, start_pair(0, k_hbm, k_s, 1, v_hbm, v_s), 0)
-
-    barrier = pltpu.get_barrier_semaphore()
-    for d in range(1, GROUP):
-        pl.semaphore_signal(
-            barrier, inc=1, device_id={"seq": plane * GROUP + (r + d) % GROUP}, device_id_type=MESH
-        )
-
-    @pl.when(plane > 0)
-    def _():
-        pl.semaphore_signal(barrier, inc=1, device_id={"seq": me - GROUP}, device_id_type=MESH)
+    lax.fori_loop(0, loads, fetch(k_hbm, v_hbm, kv_s, kv_sem), 0)
 
     gain_copy.start()
-    lax.fori_loop(0, chunks, start_pair(2, q_hbm, q_s, 3, g_hbm, g_s), 0)
+    lax.fori_loop(0, loads, fetch(q_hbm, g_hbm, qg_s, qg_sem), 0)
 
     if heads < D:
         ld_s[pl.ds(heads, D - heads)] = jnp.zeros((D - heads, tok), BF16)
@@ -126,10 +130,8 @@
     total = cumt[:, tok - 1:tok]
     kwt_s[...] = closing * jnp.exp(total - cumt)
 
-    def updates(j):
-        for yh in range(2):
-            load(0, k_hbm, k_s, j, yh).wait()
-            load(1, v_hbm, v_s, j, yh).wait()
+    def updates(u):
+        fetched(kv_s, kv_sem, u)
 
     def update_math(j):
         for yh in range(2):
@@ -142,19 +144,19 @@
                 u_own[j, hh // w, yh, hh % w] = up.astype(BF16)
 
     def core_copy(j):
-        return send(u_own.at[j, 1 - c], u_core.at[j], core_ss.at[j], core_rs.at[j], core_peer)
+        return send(u_own.at[j, 1 - c], u_core.at[j], core_ss, core_rs.at[j], core_peer)
 
     def pair_copy(j):
-        return send(u_send.at[j], u_pair.at[j], pair_ss.at[j], pair_rs.at[j], pair_peer)
+        return send(u_send.at[j], u_pair.at[j], pair_ss, pair_rs.at[j], pair_peer)
 
     def z_copy(j):
-        return send(s_out.at[j], s_in.at[j], z_ss.at[j], z_rs.at[j], (me + GROUP) % n)
+        return send(s_out.at[j], s_in.at[j], z_ss, z_rs.at[j], (me + GROUP) % n)
 
     def e_copy(j):
-        return send(e_send.at[j], e_half.at[j, y], e_ss.at[j], e_rs.at[j], pair_peer)
+        return send(e_send.at[j], e_half.at[j, y], e_ss, e_rs.at[j], pair_peer)
 
     def x_copy(j):
-        return send(x_send.at[j], ent.at[j, c], x_ss.at[j], x_rs.at[j], core_peer)
+        return send(x_send.at[j], ent.at[j, c], x_ss, x_rs.at[j], core_peer)
 
     def fac_core_copy():
         return send(fac_own, fac_core, fac_ss.at[0], fac_rs.at[0], core_peer)
@@ -188,7 +190,7 @@
         dev, off = fin_place(j, s)
         return send(
             s_out.at[j, pl.ds(s * g, g)], fin_s.at[pl.ds(off, g)],
-            f_ss.at[j, s], f_rs.at[off // g], dev,
+            f_ss, f_rs.at[off // g], dev,
         )
 
     def fin_local(j, s):
@@ -196,6 +198,10 @@
         return pltpu.make_async_copy(s_out.at[j, pl.ds(s * g, g)], fin_s.at[pl.ds(off, g)], f_ls)
 
     def chain(j):
+        @pl.when(j == 0)
+        def _():
+            fac_pair_copy().wait_recv()
+
         pair_copy(j).wait_recv()
 
         @pl.when(plane > 0)
@@ -235,16 +241,19 @@
                     fin_local(j, s).wait()
 
     def inside_wait(i):
-        load(2, q_hbm, q_s, i // 2, i % 2).wait()
-        load(3, g_hbm, g_s, i // 2, i % 2).wait()
-
-    def inside(i):
-        j = i // 2
-        yh = i % 2
-        h0 = head0(j, yh)
+        @pl.when((i % 2 == 0) & (i < 2 * loads))
+        def _():
+            fetched(qg_s, qg_sem, i // 2)
+
+    def place(i):
+        j = (i // 2) * per
+        return j, i % 2, head0(j, i % 2)
+
+    def weigh(i):
+        j, yh, h0 = place(i)
         blk = tok // 2
         cols = pltpu.roll(cum_s[...], (D - h0) % D, 1)
-        for hh in range(half):
+        for hh in range(half * per):
             at = hcol(j, yh, hh)
             row = cumt_s[pl.ds(h0 + hh, 1), :]
             kt = kt_s[h0 + hh]
@@ -253,9 +262,14 @@
             bot = dot(q_s[blk:, at], kt, ((1,), (0,)))
             top = (top * jnp.exp2((ci[:blk] - row[:, :blk]) + pen_s[:blk, :blk])).astype(BF16)
             bot = (bot * jnp.exp2((ci[blk:] - row) + pen_s[blk:, :])).astype(BF16)
-            top = jnp.concatenate([top, jnp.zeros_like(top)], axis=1)
-            wt = jnp.concatenate([top, bot], axis=0)
-            mix_s[:, at] = dot(wt, v_s[:, at], ((1,), (0,)))
+            wt_s[hh, :blk, :blk] = top
+            wt_s[hh, blk:, :] = bot
+
+    def apply(i):
+        j, yh, h0 = place(i)
+        for hh in range(half * per):
+            at = hcol(j, yh, hh)
+            mix_s[:, at] = dot(wt_s[hh], v_s[:, at], ((1,), (0,)))
             hg = 0.5 * gain_s[:, at]
             gate_s[:, at] = hg * jnp.tanh(0.5 * g_s[:, at].astype(F32)) + hg
 
@@ -272,37 +286,23 @@
                 x_send[j, yo, k] = jnp.where(c == 0, second, first)
         x_copy(j).start()
 
-    def across(j):
-        core_copy(j).wait_send()
-        pair_copy(j).wait_send()
-        e_copy(j).wait_send()
-
-        @pl.when(plane < planes - 1)
-        def _():
-            z_copy(j).wait_send()
-
-        @pl.when(plane == planes - 1)
-        def _():
-            for s in range(w // g):
-                dev, _off = fin_place(j, s)
-
-                @pl.when(dev != me)
-                def _():
-                    fin_copy(j, s).wait_send()
-
-        x_copy(j).wait_recv()
-        x_copy(j).wait_send()
+    def across_wait(a):
+        for b in range(per):
+            x_copy(a * per + b).wait_recv()
+
+    def across(a):
+        j = a * per
         cols = pltpu.roll(lead_s[...], (D - head0(j, 0)) % D, 1)
+        acc = ssq_s[...]
         for yh in range(2):
-            acc = ssq_s[...]
-            for hh in range(half):
+            for hh in range(half * per):
                 at = hcol(j, yh, hh)
                 lane = yh * span + hh
-                st = ent[j, hh // w, yh, hh % w]
+                st = ent[j + hh // half, (hh % half) // w, yh, hh % w]
                 mixed = mix_s[:, at] + cols[:, lane:lane + 1] * dot(q_s[:, at], st, ((1,), (0,)))
                 acc = acc + mixed * mixed
                 out_s[:, at] = (mixed * gate_s[:, at]).astype(BF16)
-            ssq_s[...] = acc
+        ssq_s[...] = acc
 
     updates(0)
     update_math(0)
@@ -323,13 +323,18 @@
 
     core_copy(0).start()
     fac_core_copy().start()
+    for j in range(1, per):
+        update_math(j)
+        core_copy(j).start()
     updates(1)
-    update_math(1)
-    core_copy(1).start()
+    for j in range(per, 2 * per):
+        update_math(j)
+        core_copy(j).start()
     fac_core_copy().wait_recv()
-    combine(0)
     fac_chip[...] = fac_own[...] * fac_core[...]
     fac_pair_copy().start()
+    for j in range(per):
+        combine(j)
 
     rows = lax.broadcasted_iota(jnp.int32, (tok, D), 0)
     doc_col = jnp.zeros((tok, D), jnp.int32)
@@ -349,42 +354,77 @@
         s_in[...] = jnp.zeros_like(s_in)
 
     gain_copy.wait()
-    fac_pair_copy().wait_recv()
+    wt_s[...] = jnp.zeros_like(wt_s)
+    for j in range(per, 2 * per):
+        combine(j)
+    updates(2)
+    inside_wait(0)
+    for j in range(2 * per, 3 * per):
+        update_math(j)
+    weigh(0)
+    for j in range(2 * per, 3 * per):
+        core_copy(j).start()
 
     chain_lag = CHAIN_LAG + HOP_LAG * plane
-    e_lag = jnp.maximum(chain_lag, chunks)
+    e_lag = jnp.maximum(chain_lag, chunks + per + 1)
     spread_lag = e_lag + E_LAG
-    across_lag = spread_lag + X_LAG
-    steps = jnp.maximum(chunks + across_lag, 2 * chunks + 2)
+    across_lag = spread_lag + 2 + X_LAG
+    steps = jnp.maximum(across_lag + chunks, (2 * loads + 3) * per)
 
     def step(t, carry):
-        def at(lag, count, body):
-            @pl.when((t >= lag) & (t < lag + count))
+        def at(lag, count, body, first=0):
+            @pl.when((t >= lag + first) & (t < lag + count))
             def _():
                 body(t - lag)
 
-        at(1, chunks, combine)
+        at(per + 1, chunks, combine, 2 * per)
         at(chain_lag, chunks, chain)
         at(e_lag, chunks, lambda j: e_copy(j).start())
         at(spread_lag, chunks, spread)
 
-        @pl.when(t < chunks)
-        def _():
-            updates(t)
-            inside_wait(t - 2)
-            update_math(t)
-            inside(t - 2)
-            core_copy(t).start()
-
-        @pl.when((t >= chunks) & (t < 2 * chunks + 2))
-        def _():
-            inside_wait(t - 2)
-            inside(t - 2)
-
-        at(across_lag, chunks, across)
+        u = t // per
+        a = (t - across_lag) // per
+        even = t % per == 0
+        late = even & (u >= loads) & (u < 2 * loads + 3)
+        states = even & (t >= across_lag) & (t < across_lag + chunks)
+
+        @pl.when(even & (u < loads))
+        def _():
+            updates(u)
+            inside_wait(u - 2)
+            for j in range(per):
+                update_math(t + j)
+            apply(u - 3)
+            weigh(u - 2)
+            for j in range(per):
+                core_copy(t + j).start()
+
+        @pl.when(late)
+        def _():
+            inside_wait(u - 2)
+
+        @pl.when(states)
+        def _():
+            across_wait(a)
+
+        @pl.when(late & states)
+        def _():
+            apply(u - 3)
+            weigh(jnp.minimum(u - 2, 2 * loads - 1))
+            across(a)
+
+        @pl.when(late & jnp.logical_not(states))
+        def _():
+            apply(u - 3)
+            weigh(jnp.minimum(u - 2, 2 * loads - 1))
+
+        @pl.when(states & jnp.logical_not(late))
+        def _():
+            across(a)
+
         return carry
 
-    lax.fori_loop(2, steps, step, 0)
+    lax.fori_loop(3 * per, steps, step, 0)
 
     mean = jnp.sum(ssq_s[...], axis=1, keepdims=True) * (1.0 / (heads * D))
     ssq_s[...] = jnp.broadcast_to(lax.rsqrt(mean + EPS), (tok, D))
@@ -396,17 +436,33 @@
         @pl.when(src != me)
         def _():
             send(
-                s_out.at[0, pl.ds(0, g)], fin_s.at[pl.ds(s * g, g)], f_ss.at[0, 0], f_rs.at[s], core_peer
+                s_out.at[0, pl.ds(0, g)], fin_s.at[pl.ds(s * g, g)], f_ss, f_rs.at[s], core_peer
             ).wait_recv()
 
     fac_core_copy().wait_send()
     fac_pair_copy().wait_send()
-
-
-def finish_kernel(mix_ref, inv_ref, fin_in, out_hbm, fin_ref, buf, sem):
+    send(u_own.at[:, 1 - c], u_core, core_ss, core_rs.at[0], core_peer).wait_send()
+    send(u_send, u_pair, pair_ss, pair_rs.at[0], pair_peer).wait_send()
+    send(e_send, s_in, e_ss, e_rs.at[0], pair_peer).wait_send()
+    send(x_send, e_half, x_ss, x_rs.at[0], core_peer).wait_send()
+
+    @pl.when(plane < planes - 1)
+    def _():
+        send(s_out, s_in, z_ss, z_rs.at[0], (me + GROUP) % n).wait_send()
+
+    @pl.when(plane == planes - 1)
+    def _():
+        sent = pl.ds(0, chunks - max(1, hn // (2 * w)))
+        send(s_out.at[sent], s_in.at[sent], f_ss, f_rs.at[0], core_peer).wait_send()
+
+
+def finish_kernel(mix_ref, inv_ref, fin_in, out_hbm, fin_hbm, buf, fin_s, sem, fin_sem):
     parts = buf.shape[0]
     rows = buf.shape[1]
-    copies = []
+    fin_s[...] = fin_in[...].astype(F32)
+    fin_copy = pltpu.make_async_copy(fin_s, fin_hbm, fin_sem)
+    fin_copy.start()
+    copies = [fin_copy]
     for p in range(parts):
         at = slice(p * rows, (p + 1) * rows)
         inv = inv_ref[at, :]
@@ -416,7 +472,6 @@
         copy = pltpu.make_async_copy(buf.at[p], out_hbm.at[pl.ds(p * rows, rows)], sem.at[p])
         copy.start()
         copies.append(copy)
-    fin_ref[...] = fin_in[...].astype(F32)
     for copy in copies:
         copy.wait()
 
@@ -438,19 +493,19 @@
     fac = vm((2, 2, chunks * w, D), F32)
     scratch = [
         vm((tok, width), F32), vm((tok, width), F32),
-        vm((tok, width), BF16), vm((tok, width), BF16), vm((tok, width), BF16), vm((tok, width), BF16),
+        vm((2, tok, width), BF16), vm((2, tok, width), BF16),
         vm((heads, D, tok), BF16), vm((max(heads, D), tok), BF16), vm((1, width), F32),
         pltpu.SMEM(doc_lengths.shape, jnp.int32),
         vm((tok, tok), F32), vm((heads, tok), F32), vm((heads, tok), F32), vm((tok, D), F32), vm((tok, D), F32),
         fac, fac, fac, vm((chunks * w, D), F32),
+        vm((hc // 2 * (chunks // LOADS), tok, tok), BF16),
         vm((chunks, 2, 2, w, D, D), BF16), vm((chunks, 2, w, D, D), BF16), vm((chunks, w, D, D), F32),
         part, part, part, part, part,
         vm((chunks, 2, w, D, D), BF16), vm((chunks, 2, w, D, D), BF16),
         vm((chunks, 2, 2, w, D, D), BF16),
-        dma((4, chunks, 2)), dma((3,)), dma((2,)), dma((2,)),
-        dma((chunks,)), dma((chunks,)), dma((chunks,)), dma((chunks,)), dma((chunks,)), dma((chunks,)),
-        dma((chunks,)), dma((chunks,)), dma((chunks,)), dma((chunks,)),
-        dma((chunks, w // g)), dma((hn // g,)), dma,
+        dma((LOADS,)), dma((LOADS,)), dma((3,)), dma((2,)), dma((2,)),
+        dma, dma((chunks,)), dma, dma((chunks,)), dma, dma((chunks,)), dma, dma((chunks,)), dma, dma((chunks,)),
+        dma, dma((hn // g,)), dma,
     ]
     mixed, squares, final = pl.pallas_call(
         functools.partial(kernel, n, heads, chunks),
@@ -474,8 +529,10 @@
             jax.ShapeDtypeStruct((hn, D, D), F32),
         ),
         in_specs=[vspec, vspec, vspec],
-        out_specs=(anyspace, vspec),
-        scratch_shapes=[vm((FINISH_PARTS, rows, width), BF16), dma((FINISH_PARTS,))],
+        out_specs=(anyspace, anyspace),
+        scratch_shapes=[
+            vm((FINISH_PARTS, rows, width), BF16), vm((hn, D, D), F32), dma((FINISH_PARTS,)), dma,
+        ],
         compiler_params=pltpu.CompilerParams(vmem_limit_bytes=16 * 1024 * 1024),
     )(mixed, squares, final)
 

time: 45.9 us -> 35.9 us (0.78)
  Pallas kernels: 45.1 us -> 35.1 us
    pallas_call x1, Pallas kernels: 42.2 us -> 32.8 us  [shards(): pl.pallas_call(functools.partial(kernel, n, heads, chunks), out_shape=(pl...]
    pallas_call x1, Pallas kernels: 2.88 us -> 2.27 us  [shards(): pl.pallas_call(finish_kernel, out_shape=(jax.ShapeDtypeStruct((tok, width...]
where the time goes in v3:
time: 35.9 us; the launch traced here: 35.7 us
  Pallas kernels  35.1 us (98%)
  between operations  0.64 us (2%)
    pallas_call x1, Pallas kernels, shards(): pl.pallas_call(functools.partial(kernel, n, heads, chunks), out_shape=(pl...  32.8 us
    pallas_call x1, Pallas kernels, shards(): pl.pallas_call(finish_kernel, out_shape=(jax.ShapeDtypeStruct((tok, width...  2.27 us

profile of v3, /device:TPU:25, one launch (start us, length us, event | category | flops | bytes accessed | tf_op | source)
XLA Modules:
  0.0 35.7 jit_solution(15411064018205973781)
XLA Ops:
  0.6 32.8 %shard_map.86 = (bf16[256,8192]{1,0:T(8,128)(2,1)S(1)}, f32[256,128]{1,0:T(8,128)S(1)}, bf16[4,128,128]{2,1,0:T(8,128)(2,1)S(1)}) custom-call(bf16[256,8192]{1,0:T(8,128)(2,1)} %q_hbm.1, bf16[256,8192]{1,0:T(8,128)(2,1)} %k_hbm.1, bf16[256,8192]{1,0:T(8,128)(2,1)} %v_hbm.1, bf16[256,8192]{1,0:T(8,128)(2,1)} %g_hbm.1, bf16[64,256]{1,0:T(8,128)(2,1)} %bitcast.2, ...), custom_call_target="tpu_custom_call" | custom-call | tf_op jit(solution)/shard_map/pallas_call | solution.py:510
  33.5 2.3 %shard_map.87 = (bf16[256,8192]{1,0:T(8,128)(2,1)}, f32[4,128,128]{2,1,0:T(8,128)}) custom-call(bf16[256,8192]{1,0:T(8,128)(2,1)S(1)} %get-tuple-element.5.mix_ref, f32[256,128]{1,0:T(8,128)S(1)} %get-tuple-element.6.inv_ref, bf16[4,128,128]{2,1,0:T(8,128)(2,1)S(1)} %get-tuple-element.7.fin_in), custom_call_target="tpu_custom_call" | custom-call | tf_op jit(solution)/shard_map/pallas_call | solution.py:525

commit v4 on v3

--- a/solution.py
+++ b/solution.py
@@ -17,7 +17,8 @@
 CHAIN_LAG = 9
 HOP_LAG = 4
 E_LAG = 5
-X_LAG = 2
+X_LAG = 1
+SPREAD_EARLY = 2
 FINISH_PARTS = 8
 F32, BF16 = jnp.float32, jnp.bfloat16
 MESH = pl.DeviceIdType.MESH
@@ -25,6 +26,11 @@
 
 def dot(a, b, dims):
     return lax.dot_general(a, b, (dims, ((), ())), preferred_element_type=F32)
+
+
+def diagonal(a, b):
+    zero = jnp.zeros_like(a)
+    return jnp.concatenate([jnp.concatenate([a, zero], axis=1), jnp.concatenate([zero, b], axis=1)], axis=0)
 
 
 def kernel(
@@ -34,7 +40,7 @@
     mix_s, gate_s, kv_s, qg_s, kt_s, ld_s, gain_s, docs_s, pen_s, cumt_s, kwt_s, cum_s, lead_s,
     fac_own, fac_core, fac_chip, fac_pair, wt_s, u_own, u_core, u_mine, u_send, u_pair, s_in, s_out, e_send, e_half,
     x_send, ent,
-    kv_sem, qg_sem, small_sem, fac_ss, fac_rs, core_ss, core_rs, pair_ss, pair_rs, z_ss, z_rs, e_ss, e_rs,
+    load_sem, small_sem, fac_ss, fac_rs, core_ss, core_rs, pair_ss, pair_rs, z_ss, z_rs, e_ss, e_rs,
     x_ss, x_rs, f_ss, f_rs, f_ls,
 ):
     tok = q_hbm.shape[0]
@@ -71,12 +77,12 @@
     k_s, v_s = kv_s.at[0], kv_s.at[1]
     q_s, g_s = qg_s.at[0], qg_s.at[1]
 
-    def fetch(first, second, both, sem):
+    def fetch(first, second, both):
         def go(p, carry):
             for yh in range(2):
                 at = pl.ds(pl.multiple_of(head0(p * per, yh) * D, half * per * D), half * per * D)
-                pltpu.make_async_copy(first.at[:, at], both.at[0, :, at], sem.at[p]).start()
-                pltpu.make_async_copy(second.at[:, at], both.at[1, :, at], sem.at[p]).start()
+                pltpu.make_async_copy(first.at[:, at], both.at[0, :, at], load_sem.at[p]).start()
+                pltpu.make_async_copy(second.at[:, at], both.at[1, :, at], load_sem.at[p]).start()
             return carry
         return go
 
@@ -99,10 +105,9 @@
     gain_copy = pltpu.make_async_copy(gain_hbm, gain_s, small_sem.at[2])
     ld_copy.start()
     docs_copy.start()
-    lax.fori_loop(0, loads, fetch(k_hbm, v_hbm, kv_s, kv_sem), 0)
+    lax.fori_loop(0, loads, fetch(k_hbm, v_hbm, kv_s), 0)
 
     gain_copy.start()
-    lax.fori_loop(0, loads, fetch(q_hbm, g_hbm, qg_s, qg_sem), 0)
 
     if heads < D:
         ld_s[pl.ds(heads, D - heads)] = jnp.zeros((D - heads, tok), BF16)
@@ -131,7 +136,8 @@
     kwt_s[...] = closing * jnp.exp(total - cumt)
 
     def updates(u):
-        fetched(kv_s, kv_sem, u)
+        fetched(kv_s, load_sem, u)
+        fetch(q_hbm, g_hbm, qg_s)(u, 0)
 
     def update_math(j):
         for yh in range(2):
@@ -156,7 +162,8 @@
         return send(e_send.at[j], e_half.at[j, y], e_ss, e_rs.at[j], pair_peer)
 
     def x_copy(j):
-        return send(x_send.at[j], ent.at[j, c], x_ss, x_rs.at[j], core_peer)
+        at = pl.ds(j * per, per)
+        return send(x_send.at[at], ent.at[at, c], x_ss, x_rs.at[j], core_peer)
 
     def fac_core_copy():
         return send(fac_own, fac_core, fac_ss.at[0], fac_rs.at[0], core_peer)
@@ -243,38 +250,60 @@
     def inside_wait(i):
         @pl.when((i % 2 == 0) & (i < 2 * loads))
         def _():
-            fetched(qg_s, qg_sem, i // 2)
+            fetched(qg_s, load_sem, i // 2)
 
     def place(i):
         j = (i // 2) * per
         return j, i % 2, head0(j, i % 2)
+
+    def wide(j, yh, hh):
+        return pl.ds(pl.multiple_of((head0(j, yh) + hh) * D, 2 * D), 2 * D)
 
     def weigh(i):
         j, yh, h0 = place(i)
         blk = tok // 2
         cols = pltpu.roll(cum_s[...], (D - h0) % D, 1)
-        for hh in range(half * per):
-            at = hcol(j, yh, hh)
-            row = cumt_s[pl.ds(h0 + hh, 1), :]
-            kt = kt_s[h0 + hh]
-            ci = cols[:, hh:hh + 1]
-            top = dot(q_s[:blk, at], kt[:, :blk], ((1,), (0,)))
-            bot = dot(q_s[blk:, at], kt, ((1,), (0,)))
-            top = (top * jnp.exp2((ci[:blk] - row[:, :blk]) + pen_s[:blk, :blk])).astype(BF16)
-            bot = (bot * jnp.exp2((ci[blk:] - row) + pen_s[blk:, :])).astype(BF16)
-            wt_s[hh, :blk, :blk] = top
-            wt_s[hh, blk:, :] = bot
+        for hh in range(0, half * per, 2):
+            top = dot(
+                q_s[:blk, wide(j, yh, hh)],
+                diagonal(kt_s[h0 + hh, :, :blk], kt_s[h0 + hh + 1, :, :blk]), ((1,), (0,)),
+            )
+            for b in range(2):
+                h = hh + b
+                row = cumt_s[pl.ds(h0 + h, 1), :]
+                ci = cols[:, h:h + 1]
+                bot = dot(q_s[blk:, hcol(j, yh, h)], kt_s[h0 + h], ((1,), (0,)))
+                at = slice(b * blk, (b + 1) * blk)
+                wt_s[hh // 2, 0, :, at] = (
+                    top[:, at] * jnp.exp2((ci[:blk] - row[:, :blk]) + pen_s[:blk, :blk])
+                ).astype(BF16)
+                wt_s[hh // 2, 1 + b] = (bot * jnp.exp2((ci[blk:] - row) + pen_s[blk:, :])).astype(BF16)
 
     def apply(i):
         j, yh, h0 = place(i)
-        for hh in range(half * per):
-            at = hcol(j, yh, hh)
-            mix_s[:, at] = dot(wt_s[hh], v_s[:, at], ((1,), (0,)))
-            hg = 0.5 * gain_s[:, at]
-            gate_s[:, at] = hg * jnp.tanh(0.5 * g_s[:, at].astype(F32)) + hg
+        blk = tok // 2
+        for hh in range(0, half * per, 2):
+            both = wide(j, yh, hh)
+            mix_s[:blk, both] = dot(
+                wt_s[hh // 2, 0],
+                diagonal(v_s[:blk, hcol(j, yh, hh)], v_s[:blk, hcol(j, yh, hh + 1)]), ((1,), (0,)),
+            )
+            for b in range(2):
+                at = hcol(j, yh, hh + b)
+                mix_s[blk:, at] = dot(wt_s[hh // 2, 1 + b], v_s[:, at], ((1,), (0,)))
+            hg = 0.5 * gain_s[:, both]
+            gate_s[:, both] = hg * jnp.tanh(0.5 * g_s[:, both].astype(F32)) + hg
+
+    def share(j):
+        @pl.when((plane > 0) | (y == 0))
+        def _():
+            e_copy(j).start()
 
     def spread(j):
-        e_copy(j).wait_recv()
+        @pl.when((plane > 0) | (y == 1))
+        def _():
+            e_copy(j).wait_recv()
+
         for yo in range(2):
             for k in range(w):
                 at = pl.ds(j * w + k, 1)
@@ -284,24 +313,28 @@
                 second = (f0 * first.astype(F32) + u0).astype(BF16)
                 ent[j, c, yo, k] = jnp.where(c == 0, first, second)
                 x_send[j, yo, k] = jnp.where(c == 0, second, first)
-        x_copy(j).start()
+
+        @pl.when(j % per == per - 1)
+        def _():
+            x_copy(j // per).start()
 
     def across_wait(a):
-        for b in range(per):
-            x_copy(a * per + b).wait_recv()
+        x_copy(a).wait_recv()
 
     def across(a):
         j = a * per
         cols = pltpu.roll(lead_s[...], (D - head0(j, 0)) % D, 1)
         acc = ssq_s[...]
         for yh in range(2):
-            for hh in range(half * per):
-                at = hcol(j, yh, hh)
-                lane = yh * span + hh
-                st = ent[j + hh // half, (hh % half) // w, yh, hh % w]
-                mixed = mix_s[:, at] + cols[:, lane:lane + 1] * dot(q_s[:, at], st, ((1,), (0,)))
-                acc = acc + mixed * mixed
-                out_s[:, at] = (mixed * gate_s[:, at]).astype(BF16)
+            for hh in range(0, half * per, 2):
+                entry = [ent[j + h // half, (h % half) // w, yh, h % w] for h in (hh, hh + 1)]
+                both = dot(q_s[:, wide(j, yh, hh)], diagonal(*entry), ((1,), (0,)))
+                for b in range(2):
+                    at = hcol(j, yh, hh + b)
+                    lane = yh * span + hh + b
+                    mixed = mix_s[:, at] + cols[:, lane:lane + 1] * both[:, b * D:(b + 1) * D]
+                    acc = acc + mixed * mixed
+                    out_s[:, at] = (mixed * gate_s[:, at]).astype(BF16)
         ssq_s[...] = acc
 
     updates(0)
@@ -353,8 +386,11 @@
     def _():
         s_in[...] = jnp.zeros_like(s_in)
 
+    @pl.when((plane == 0) & (y == 0))
+    def _():
+        e_half[:, 1] = jnp.zeros(e_half.shape[:1] + e_half.shape[2:], BF16)
+
     gain_copy.wait()
-    wt_s[...] = jnp.zeros_like(wt_s)
     for j in range(per, 2 * per):
         combine(j)
     updates(2)
@@ -365,10 +401,11 @@
     for j in range(2 * per, 3 * per):
         core_copy(j).start()
 
-    chain_lag = CHAIN_LAG + HOP_LAG * plane
+    chain_lag = 9 + 4 * plane + 2 * (plane // (planes - 1))
     e_lag = jnp.maximum(chain_lag, chunks + per + 1)
-    spread_lag = e_lag + E_LAG
-    across_lag = spread_lag + 2 + X_LAG
+    ends = jnp.where(plane == planes - 1, 0, chain_lag + chunks - SPREAD_EARLY)
+    spread_lag = jnp.maximum(e_lag + E_LAG, ends)
+    across_lag = (spread_lag + X_LAG + 2) // 2 * 2 + 1
     steps = jnp.maximum(across_lag + chunks, (2 * loads + 3) * per)
 
     def step(t, carry):
@@ -379,14 +416,14 @@
 
         at(per + 1, chunks, combine, 2 * per)
         at(chain_lag, chunks, chain)
-        at(e_lag, chunks, lambda j: e_copy(j).start())
+        at(e_lag, chunks, share)
         at(spread_lag, chunks, spread)
 
         u = t // per
         a = (t - across_lag) // per
         even = t % per == 0
-        late = even & (u >= loads) & (u < 2 * loads + 3)
-        states = even & (t >= across_lag) & (t < across_lag + chunks)
+        odd = t % per == 1
+        states = odd & (t >= across_lag) & (t < across_lag + chunks)
 
         @pl.when(even & (u < loads))
         def _():
@@ -399,27 +436,21 @@
             for j in range(per):
                 core_copy(t + j).start()
 
-        @pl.when(late)
-        def _():
-            inside_wait(u - 2)
+        i = t - chunks + loads - 2
+
+        @pl.when((t >= chunks) & (i < 2 * loads))
+        def _():
+            inside_wait(i)
+            apply(i - 1)
+            weigh(i)
+
+        @pl.when(i == 2 * loads)
+        def _():
+            apply(i - 1)
 
         @pl.when(states)
         def _():
             across_wait(a)
-
-        @pl.when(late & states)
-        def _():
-            apply(u - 3)
-            weigh(jnp.minimum(u - 2, 2 * loads - 1))
-            across(a)
-
-        @pl.when(late & jnp.logical_not(states))
-        def _():
-            apply(u - 3)
-            weigh(jnp.minimum(u - 2, 2 * loads - 1))
-
-        @pl.when(states & jnp.logical_not(late))
-        def _():
             across(a)
 
         return carry
@@ -443,7 +474,11 @@
     fac_pair_copy().wait_send()
     send(u_own.at[:, 1 - c], u_core, core_ss, core_rs.at[0], core_peer).wait_send()
     send(u_send, u_pair, pair_ss, pair_rs.at[0], pair_peer).wait_send()
-    send(e_send, s_in, e_ss, e_rs.at[0], pair_peer).wait_send()
+
+    @pl.when((plane > 0) | (y == 0))
+    def _():
+        send(e_send, s_in, e_ss, e_rs.at[0], pair_peer).wait_send()
+
     send(x_send, e_half, x_ss, x_rs.at[0], core_peer).wait_send()
 
     @pl.when(plane < planes - 1)
@@ -498,13 +533,13 @@
         pltpu.SMEM(doc_lengths.shape, jnp.int32),
         vm((tok, tok), F32), vm((heads, tok), F32), vm((heads, tok), F32), vm((tok, D), F32), vm((tok, D), F32),
         fac, fac, fac, vm((chunks * w, D), F32),
-        vm((hc // 2 * (chunks // LOADS), tok, tok), BF16),
+        vm((hc // 4 * (chunks // LOADS), 3, tok // 2, tok), BF16),
         vm((chunks, 2, 2, w, D, D), BF16), vm((chunks, 2, w, D, D), BF16), vm((chunks, w, D, D), F32),
         part, part, part, part, part,
         vm((chunks, 2, w, D, D), BF16), vm((chunks, 2, w, D, D), BF16),
         vm((chunks, 2, 2, w, D, D), BF16),
-        dma((LOADS,)), dma((LOADS,)), dma((3,)), dma((2,)), dma((2,)),
-        dma, dma((chunks,)), dma, dma((chunks,)), dma, dma((chunks,)), dma, dma((chunks,)), dma, dma((chunks,)),
+        dma((LOADS,)), dma((3,)), dma((2,)), dma((2,)),
+        dma, dma((chunks,)), dma, dma((chunks,)), dma, dma((chunks,)), dma, dma((chunks,)), dma, dma((LOADS,)),
         dma, dma((hn // g,)), dma,
     ]
     mixed, squares, final = pl.pallas_call(

time: 35.9 us -> 34.7 us (0.967)
  Pallas kernels: 35.1 us -> 34 us
    pallas_call x1, Pallas kernels: 32.8 us -> 31.7 us  [shards(): pl.pallas_call(functools.partial(kernel, n, heads, chunks), out_shape=(pl...]
where the time goes in v4:
time: 34.7 us; the launch traced here: 34.6 us
  Pallas kernels  34 us (98%)
  between operations  0.64 us (2%)
    pallas_call x1, Pallas kernels, shards(): pl.pallas_call(functools.partial(kernel, n, heads, chunks), out_shape=(pl...  31.7 us
    pallas_call x1, Pallas kernels, shards(): pl.pallas_call(finish_kernel, out_shape=(jax.ShapeDtypeStruct((tok, width...  2.27 us

profile of v4, /device:TPU:25, one launch (start us, length us, event | category | flops | bytes accessed | tf_op | source)
XLA Modules:
  0.0 34.6 jit_solution(11873101902939006322)
XLA Ops:
  0.6 31.7 %shard_map.86 = (bf16[256,8192]{1,0:T(8,128)(2,1)S(1)}, f32[256,128]{1,0:T(8,128)S(1)}, bf16[4,128,128]{2,1,0:T(8,128)(2,1)S(1)}) custom-call(bf16[256,8192]{1,0:T(8,128)(2,1)} %q_hbm.1, bf16[256,8192]{1,0:T(8,128)(2,1)} %k_hbm.1, bf16[256,8192]{1,0:T(8,128)(2,1)} %v_hbm.1, bf16[256,8192]{1,0:T(8,128)(2,1)} %g_hbm.1, bf16[64,256]{1,0:T(8,128)(2,1)} %bitcast.2, ...), custom_call_target="tpu_custom_call" | custom-call | tf_op jit(solution)/shard_map/pallas_call | solution.py:545
  32.3 2.3 %shard_map.87 = (bf16[256,8192]{1,0:T(8,128)(2,1)}, f32[4,128,128]{2,1,0:T(8,128)}) custom-call(bf16[256,8192]{1,0:T(8,128)(2,1)S(1)} %get-tuple-element.5.mix_ref, f32[256,128]{1,0:T(8,128)S(1)} %get-tuple-element.6.inv_ref, bf16[4,128,128]{2,1,0:T(8,128)(2,1)S(1)} %get-tuple-element.7.fin_in), custom_call_target="tpu_custom_call" | custom-call | tf_op jit(solution)/shard_map/pallas_call | solution.py:560

commit v5 on v4

--- a/solution.py
+++ b/solution.py
@@ -18,7 +18,7 @@
 HOP_LAG = 4
 E_LAG = 5
 X_LAG = 1
-SPREAD_EARLY = 2
+SPREAD_EARLY = 8
 FINISH_PARTS = 8
 F32, BF16 = jnp.float32, jnp.bfloat16
 MESH = pl.DeviceIdType.MESH

time: 34.7 us -> 34.7 us (level)
  no operation moved by 1% of the time
where the time goes in v5:
time: 34.7 us; the launch traced here: 34.6 us
  Pallas kernels  34 us (98%)
  between operations  0.64 us (2%)
    pallas_call x1, Pallas kernels, shards(): pl.pallas_call(functools.partial(kernel, n, heads, chunks), out_shape=(pl...  31.7 us
    pallas_call x1, Pallas kernels, shards(): pl.pallas_call(finish_kernel, out_shape=(jax.ShapeDtypeStruct((tok, width...  2.27 us

profile of v5, /device:TPU:25, one launch (start us, length us, event | category | flops | bytes accessed | tf_op | source)
XLA Modules:
  0.0 34.6 jit_solution(16498039967299231167)
XLA Ops:
  0.6 31.7 %shard_map.86 = (bf16[256,8192]{1,0:T(8,128)(2,1)S(1)}, f32[256,128]{1,0:T(8,128)S(1)}, bf16[4,128,128]{2,1,0:T(8,128)(2,1)S(1)}) custom-call(bf16[256,8192]{1,0:T(8,128)(2,1)} %q_hbm.1, bf16[256,8192]{1,0:T(8,128)(2,1)} %k_hbm.1, bf16[256,8192]{1,0:T(8,128)(2,1)} %v_hbm.1, bf16[256,8192]{1,0:T(8,128)(2,1)} %g_hbm.1, bf16[64,256]{1,0:T(8,128)(2,1)} %bitcast.2, ...), custom_call_target="tpu_custom_call" | custom-call | tf_op jit(solution)/shard_map/pallas_call | solution.py:545
  32.3 2.3 %shard_map.87 = (bf16[256,8192]{1,0:T(8,128)(2,1)}, f32[4,128,128]{2,1,0:T(8,128)}) custom-call(bf16[256,8192]{1,0:T(8,128)(2,1)S(1)} %get-tuple-element.5.mix_ref, f32[256,128]{1,0:T(8,128)S(1)} %get-tuple-element.6.inv_ref, bf16[4,128,128]{2,1,0:T(8,128)(2,1)S(1)} %get-tuple-element.7.fin_in), custom_call_target="tpu_custom_call" | custom-call | tf_op jit(solution)/shard_map/pallas_call | solution.py:560

commit v6 on v5

--- a/solution.py
+++ b/solution.py
@@ -14,6 +14,7 @@
 GROUP = 4
 CHUNKS = 16
 LOADS = 8
+AHEAD = 3
 CHAIN_LAG = 9
 HOP_LAG = 4
 E_LAG = 5
@@ -90,6 +91,11 @@
         part = both.at[:, :, pl.ds(0, 2 * half * per * D)]
         pltpu.make_async_copy(part, part, sem.at[p]).wait()
 
+    ld_copy = pltpu.make_async_copy(ld_hbm, ld_s.at[pl.ds(0, heads)], small_sem.at[0])
+    docs_copy = pltpu.make_async_copy(docs_hbm, docs_s, small_sem.at[1])
+    gain_copy = pltpu.make_async_copy(gain_hbm, gain_s, small_sem.at[2])
+    ld_copy.start()
+    docs_copy.start()
     barrier = pltpu.get_barrier_semaphore()
     for d in range(1, GROUP):
         pl.semaphore_signal(
@@ -100,12 +106,7 @@
     def _():
         pl.semaphore_signal(barrier, inc=1, device_id={"seq": me - GROUP}, device_id_type=MESH)
 
-    ld_copy = pltpu.make_async_copy(ld_hbm, ld_s.at[pl.ds(0, heads)], small_sem.at[0])
-    docs_copy = pltpu.make_async_copy(docs_hbm, docs_s, small_sem.at[1])
-    gain_copy = pltpu.make_async_copy(gain_hbm, gain_s, small_sem.at[2])
-    ld_copy.start()
-    docs_copy.start()
-    lax.fori_loop(0, loads, fetch(k_hbm, v_hbm, kv_s), 0)
+    lax.fori_loop(0, AHEAD, fetch(k_hbm, v_hbm, kv_s), 0)
 
     gain_copy.start()
 
@@ -138,6 +139,10 @@
     def updates(u):
         fetched(kv_s, load_sem, u)
         fetch(q_hbm, g_hbm, qg_s)(u, 0)
+
+        @pl.when(u + AHEAD < loads)
+        def _():
+            fetch(k_hbm, v_hbm, kv_s)(u + AHEAD, 0)
 
     def update_math(j):
         for yh in range(2):

time: 34.7 us -> 34.5 us (level)
  Pallas kernels: 34 us -> 33.5 us
    pallas_call x1, Pallas kernels: 31.7 us -> 31.2 us  [shards(): pl.pallas_call(functools.partial(kernel, n, heads, chunks), out_shape=(pl...]
where the time goes in v6:
time: 34.5 us; the launch traced here: 34.2 us
  Pallas kernels  33.5 us (97%)
  between operations  0.64 us (2%)
    pallas_call x1, Pallas kernels, shards(): pl.pallas_call(functools.partial(kernel, n, heads, chunks), out_shape=(pl...  31.2 us
    pallas_call x1, Pallas kernels, shards(): pl.pallas_call(finish_kernel, out_shape=(jax.ShapeDtypeStruct((tok, width...  2.27 us

profile of v6, /device:TPU:25, one launch (start us, length us, event | category | flops | bytes accessed | tf_op | source)
XLA Modules:
  0.0 34.2 jit_solution(11293584524313159272)
XLA Ops:
  0.6 31.2 %shard_map.86 = (bf16[256,8192]{1,0:T(8,128)(2,1)S(1)}, f32[256,128]{1,0:T(8,128)S(1)}, bf16[4,128,128]{2,1,0:T(8,128)(2,1)S(1)}) custom-call(bf16[256,8192]{1,0:T(8,128)(2,1)} %q_hbm.1, bf16[256,8192]{1,0:T(8,128)(2,1)} %k_hbm.1, bf16[256,8192]{1,0:T(8,128)(2,1)} %v_hbm.1, bf16[256,8192]{1,0:T(8,128)(2,1)} %g_hbm.1, bf16[64,256]{1,0:T(8,128)(2,1)} %bitcast.2, ...), custom_call_target="tpu_custom_call" | custom-call | tf_op jit(solution)/shard_map/pallas_call | solution.py:550
  31.9 2.3 %shard_map.87 = (bf16[256,8192]{1,0:T(8,128)(2,1)}, f32[4,128,128]{2,1,0:T(8,128)}) custom-call(bf16[256,8192]{1,0:T(8,128)(2,1)S(1)} %get-tuple-element.5.mix_ref, f32[256,128]{1,0:T(8,128)S(1)} %get-tuple-element.6.inv_ref, bf16[4,128,128]{2,1,0:T(8,128)(2,1)S(1)} %get-tuple-element.7.fin_in), custom_call_target="tpu_custom_call" | custom-call | tf_op jit(solution)/shard_map/pallas_call | solution.py:565

commit v7 on v6

--- a/solution.py
+++ b/solution.py
@@ -14,7 +14,7 @@
 GROUP = 4
 CHUNKS = 16
 LOADS = 8
-AHEAD = 3
+AHEAD = 2
 CHAIN_LAG = 9
 HOP_LAG = 4
 E_LAG = 5

time: 34.5 us -> 34.5 us (level)
  no operation moved by 1% of the time
where the time goes in v7:
time: 34.5 us; the launch traced here: 34.2 us
  Pallas kernels  33.5 us (97%)
  between operations  0.64 us (2%)
    pallas_call x1, Pallas kernels, shards(): pl.pallas_call(functools.partial(kernel, n, heads, chunks), out_shape=(pl...  31.2 us
    pallas_call x1, Pallas kernels, shards(): pl.pallas_call(finish_kernel, out_shape=(jax.ShapeDtypeStruct((tok, width...  2.27 us

profile of v7, /device:TPU:25, one launch (start us, length us, event | category | flops | bytes accessed | tf_op | source)
XLA Modules:
  0.0 34.2 jit_solution(16514380583999694776)
XLA Ops:
  0.6 31.2 %shard_map.86 = (bf16[256,8192]{1,0:T(8,128)(2,1)S(1)}, f32[256,128]{1,0:T(8,128)S(1)}, bf16[4,128,128]{2,1,0:T(8,128)(2,1)S(1)}) custom-call(bf16[256,8192]{1,0:T(8,128)(2,1)} %q_hbm.1, bf16[256,8192]{1,0:T(8,128)(2,1)} %k_hbm.1, bf16[256,8192]{1,0:T(8,128)(2,1)} %v_hbm.1, bf16[256,8192]{1,0:T(8,128)(2,1)} %g_hbm.1, bf16[64,256]{1,0:T(8,128)(2,1)} %bitcast.2, ...), custom_call_target="tpu_custom_call" | custom-call | tf_op jit(solution)/shard_map/pallas_call | solution.py:550
  31.9 2.3 %shard_map.87 = (bf16[256,8192]{1,0:T(8,128)(2,1)}, f32[4,128,128]{2,1,0:T(8,128)}) custom-call(bf16[256,8192]{1,0:T(8,128)(2,1)S(1)} %get-tuple-element.5.mix_ref, f32[256,128]{1,0:T(8,128)S(1)} %get-tuple-element.6.inv_ref, bf16[4,128,128]{2,1,0:T(8,128)(2,1)S(1)} %get-tuple-element.7.fin_in), custom_call_target="tpu_custom_call" | custom-call | tf_op jit(solution)/shard_map/pallas_call | solution.py:565
